TPU v7x, 32 devices: a whole 2x2x4 slice. The times are simulated.
32 devices in a mesh: img: 8 (over z, y), grp: 4 (over x, core).
Axes of the slice: x: 2, y: 2, z: 4, core: 2. Of those that a mesh axis runs over, the one named last changes fastest.
Arguments:
- images: bfloat16 [12288, 9216], P(('img', 'grp')), may hold values from -64 to 64, as said below
- expansion_basis: bfloat16 [9216, 960], P(None, 'img'), may hold values from -0.0625 to 0.0625
- block_sizes: int32 [16], replicated, may hold values from 1 to 80, 480 in all
- keep_count: int32 [16], replicated, may hold values from 1 to 8
- start_block: float32 [16, 80, 8], replicated, may hold values from -6 to 6
Outputs:
- features: float32 [12288, 256], P(('img', 'grp'))
- values: float32 [16, 8], replicated
Inputs may be any that keep to these rules, and one draw needn't show every extreme that they name: `images`: pixel values of order one. `block_sizes`: the 16 sizes sum to 480.
All inputs are finite; a program needn't handle non-finite values.
Results may differ from a plain program's by a relative error of at most 0.025.
Values may be sent and summed in bfloat16 or wider, within the bound.
No kernel may reach another device: no remote copies, remote signals or barrier semaphores. Data moves between devices by JAX's collectives and lax.ppermute only.
A program may use at most 128 MiB of HBM per device.

v0:
```python
import jax
import jax.numpy as jnp
from jax import lax
from jax.sharding import PartitionSpec as P

NMAX = 80
L = 16
S = 480
KMAX = 8
ITERS = 3
HIGH = lax.Precision.HIGHEST


def selector(block_sizes, total, count, width):
    offsets = jnp.cumsum(block_sizes) - block_sizes
    column = jnp.arange(total, dtype=jnp.int32)[:, None, None]
    inside = jnp.arange(width, dtype=jnp.int32)[None, None, :]
    hit = (column == offsets[None, :, None] + inside) & (inside < block_sizes[None, :, None])
    return hit.astype(jnp.bfloat16).reshape(total, count * width)


def subspace(cover, block_sizes, keep_count, start_block):
    width = cover.shape[1]
    ranks = start_block.shape[2]
    inside = jnp.arange(width, dtype=jnp.int32)[None, :, None] < block_sizes[:, None, None]
    keep = jnp.minimum(keep_count, (block_sizes + 1) // 2)
    current = jnp.where(inside, start_block, jnp.zeros_like(start_block))
    for turn in range(ITERS):
        product = jnp.einsum("bij,bjk->bik", cover, current, precision=HIGH)
        columns = []
        for column_id in range(ranks):
            vector = product[:, :, column_id]
            for earlier in columns:
                vector = vector - jnp.sum(earlier * vector, axis=1, keepdims=True) * earlier
            length = jnp.sqrt(jnp.sum(vector * vector, axis=1, keepdims=True))
            alive = (column_id < keep)[:, None]
            columns.append(jnp.where(alive, vector / length, jnp.zeros_like(vector)))
        current = jnp.stack(columns, axis=2)
    product = jnp.einsum("bij,bjk->bik", cover, current, precision=HIGH)
    found = jnp.sum(current * product, axis=1)
    return (current, found)


def spread(partial_value, block_sizes, keep_count, start_block, owners, owner):
    slots = -(-partial_value.shape[0] // owners)
    extra = slots * owners - partial_value.shape[0]
    stacked = jnp.pad(partial_value, ((0, extra), (0, 0), (0, 0)))
    first = owner * slots
    mine_sizes = lax.dynamic_slice_in_dim(jnp.pad(block_sizes, (0, extra)), first, slots)
    mine_keep = lax.dynamic_slice_in_dim(jnp.pad(keep_count, (0, extra)), first, slots)
    mine_start = lax.dynamic_slice_in_dim(
        jnp.pad(start_block, ((0, extra), (0, 0), (0, 0))), first, slots
    )
    return (stacked, mine_sizes, mine_keep, mine_start)


def per_device(images, expansion_basis, block_sizes, keep_count, start_block):
    rows = images.shape[0]
    coeffs = jnp.dot(
        images,
        lax.all_gather(expansion_basis, "img", axis=1, tiled=True),
        preferred_element_type=jnp.float32,
    ).astype(jnp.bfloat16)
    samples = coeffs.reshape(2 * rows, S)
    pick = selector(block_sizes, S, L, NMAX)
    padded = jnp.dot(samples, pick, preferred_element_type=jnp.float32).astype(jnp.bfloat16)
    wide = padded.reshape(2 * rows, L, NMAX)
    scale = 1.0 / (2 * rows * lax.axis_size("img") * lax.axis_size("grp"))
    partial_value = (
        jnp.einsum("rli,rlj->lij", wide, wide, preferred_element_type=jnp.float32) * scale
    )
    stacked, mine_sizes, mine_keep, mine_start = spread(
        partial_value,
        block_sizes,
        keep_count,
        start_block,
        lax.axis_size(("img", "grp")),
        lax.axis_index(("img", "grp")),
    )
    owned = lax.psum_scatter(stacked, ("img", "grp"), scatter_dimension=0, tiled=True)
    solved, quotients = subspace(owned, mine_sizes, mine_keep, mine_start)
    vectors, found = (
        lax.all_gather(solved, ("img", "grp"), axis=0, tiled=True),
        lax.all_gather(quotients, ("img", "grp"), axis=0, tiled=True),
    )
    vectors = vectors[:L]
    found = found[:L]
    rounded = vectors.astype(jnp.bfloat16)
    features = jnp.einsum("rli,lij->rlj", wide, rounded, preferred_element_type=jnp.float32)
    return (features.reshape(rows, 2 * L * KMAX), found)


def solution(mesh):
    in_specs = (P(("img", "grp"), None), P(None, "img"), P(), P(), P())
    out_specs = (P(("img", "grp"), None), P())
    return jax.shard_map(
        per_device, mesh=mesh, in_specs=in_specs, out_specs=out_specs, check_vma=False
    )
```

profile of v0, /device:TPU:14, one launch (start us, length us, event | category | flops | bytes accessed | tf_op | source)
XLA Modules:
  0.0 784.9 jit_solution(9824263346163303519)
XLA Ops:
  8.6 341.4 %all-gather.3.cloned.1.call-done = bf16[9216,960]{0,1:T(8,128)(2,1)} async-done(((bf16[9216,120]{0,1:T(8,128)(2,1)}), bf16[9216,960]{0,1:T(8,128)(2,1)}) %all-gather.3.cloned.1.call-update) | async-done | bytes 17694736 | tf_op jit(solution)/shard_map/all_gather | solution.py:61
  350.0 15.1 %convolution_convert_fusion.1 = bf16[384,960]{0,1:T(8,128)(2,1)S(1)} fusion(bf16[384,9216]{1,0:T(8,128)(2,1)} %param.5, bf16[9216,960]{0,1:T(8,128)(2,1)} %all-gather.3.cloned.1.call-done), kind=kOutput, calls=%fused_computation.3 | convolution fusion | flops 6795141120 | bytes 25509888 | tf_op jit(solution)/shard_map/dot_general | solution.py:59
  365.9 2.5 convolution_convert_fusion
  368.5 2.7 copy.19
  382.7 96.0 %reduce-scatter.2.cloned.1.call-done = f32[1,80,80]{2,1,0:T(8,128)} async-done(((f32[32,80,80]{2,1,0:T(8,128)}), f32[1,80,80]{2,1,0:T(8,128)}) %reduce-scatter.2.cloned.1.call-update) | async-done | bytes 25616 | tf_op jit(solution)/shard_map/reduce_scatter | solution.py:80
  483.6 2.0 multiply_reduce_fusion.84
  485.5 4.4 multiply_reduce_fusion.64
  490.6 4.4 multiply_reduce_fusion.63
  495.0 1.9 multiply_reduce_fusion.80
  497.6 1.9 multiply_reduce_fusion.77
  499.5 5.0 multiply_reduce_fusion.62
  505.2 3.2 multiply_reduce_fusion.61
  508.4 1.9 multiply_reduce_fusion.71
  511.0 1.7 multiply_reduce_fusion.66
  512.7 2.6 multiply_reduce_fusion.60
  516.0 1.9 multiply_reduce_fusion.59
  517.9 1.9 multiply_reduce_fusion.58
  520.5 17.5 %broadcast_select_fusion.5 = (f32[1,80,1]{1,2,0:T(1,128)S(1)}, f32[1,80,1]{1,2,0:T(1,128)S(1)}, f32[1,80,1]{1,2,0:T(1,128)S(1)}, f32[1,80,1]{1,2,0:T(1,128)S(1)}...) fusion(pred[]{:T(512)} %bitcast.20, f32[1,80,1]{1,2,0:T(1,128)S(1)} %get-tuple-element.193, ...), kind=kLoop, calls=%fused_computation.33 | loop fusion | flops 5600 | bytes 4947 | tf_op jit(solution)/shard_map/jit(_where)/select_n | solution.py:37
  542.9 2.0 multiply_reduce_fusion.55
  544.9 4.4 multiply_reduce_fusion.35
  549.9 4.4 multiply_reduce_fusion.34
  554.3 1.9 multiply_reduce_fusion.51
  556.9 1.9 multiply_reduce_fusion.48
  558.8 5.0 multiply_reduce_fusion.33
  564.6 3.2 multiply_reduce_fusion.32
  567.7 1.9 multiply_reduce_fusion.42
  570.4 1.7 multiply_reduce_fusion.37
  572.1 2.6 multiply_reduce_fusion.31
  575.4 1.9 multiply_reduce_fusion.30
  577.3 1.9 multiply_reduce_fusion.29
  579.9 17.5 %broadcast_select_fusion.4 = (f32[1,80,1]{1,2,0:T(1,128)S(1)}, f32[1,80,1]{1,2,0:T(1,128)S(1)}, f32[1,80,1]{1,2,0:T(1,128)S(1)}, f32[1,80,1]{1,2,0:T(1,128)S(1)}...) fusion(pred[]{:T(512)} %bitcast.20, f32[1,80,1]{1,2,0:T(1,128)S(1)} %get-tuple-element.158, ...), kind=kLoop, calls=%fused_computation.32 | loop fusion | flops 5600 | bytes 4947 | tf_op jit(solution)/shard_map/jit(_where)/select_n | solution.py:37
  602.3 2.0 multiply_reduce_fusion.26
  604.3 4.4 multiply_reduce_fusion.6
  609.3 4.4 multiply_reduce_fusion.5
  613.7 1.9 multiply_reduce_fusion.22
  616.3 1.9 multiply_reduce_fusion.19
  618.2 5.0 multiply_reduce_fusion.4
  623.9 3.2 multiply_reduce_fusion.3
  627.1 1.9 multiply_reduce_fusion.13
  629.7 1.7 multiply_reduce_fusion.8
  631.5 2.6 multiply_reduce_fusion.2
  634.8 1.9 multiply_reduce_fusion.1
  636.6 1.9 multiply_reduce_fusion
  639.3 17.5 %broadcast_select_fusion.3 = (f32[1,80,1]{1,2,0:T(1,128)S(1)}, f32[1,80,1]{1,2,0:T(1,128)S(1)}, f32[1,80,1]{1,2,0:T(1,128)S(1)}, f32[1,80,1]{1,2,0:T(1,128)S(1)}...) fusion(pred[]{:T(512)} %bitcast.20, f32[1,80,1]{1,2,0:T(1,128)S(1)} %get-tuple-element.123, ...), kind=kLoop, calls=%fused_computation.31 | loop fusion | flops 5600 | bytes 4947 | tf_op jit(solution)/shard_map/jit(_where)/select_n | solution.py:37
  656.8 59.5 %all_gather.10 = bf16[32,80,8]{1,2,0:T(8,128)(2,1)S(1)} all-gather(bf16[1,80,8]{1,2,0:T(8,128)(2,1)S(1)} %convert.6), channel_id=1, replica_groups=mesh['img'=8,'grp'=4] {'img','grp'}, dimensions={0}, use_global_device_ids=true | all-gather | bytes 42240 | tf_op jit(solution)/shard_map/all_gather | solution.py:83
  716.6 4.9 copy.20
  721.5 6.3 reshape.4100
  728.4 48.9 %all-reduce.4 = f32[256]{0:T(256)S(1)} all-reduce(f32[256]{0:T(256)S(1)} %dynamic-update-slice), channel_id=2, replica_groups=mesh['img'=8,'grp'=4] {'img','grp'}, use_global_device_ids=true, to_apply=%add.4 | all-reduce | flops 256 | bytes 2048
  (54 shorter events, 18.2 us)
Async XLA Ops:
  7.2 0.8 copy-start.2
  7.2 342.9 %all-gather.3.cloned.1.call-start = ((), (), s32[]{:S(2)}) async-start(), calls=%async_computation.1 | async-start | bytes 19906560 | tf_op jit(solution)/shard_map/all_gather | solution.py:61
  7.9 470.8 %reduce-scatter.2.cloned.1.call-start = ((), (), s32[]{:S(2)}) async-start(), calls=%async_computation.2 | async-start | bytes 1351680 | tf_op jit(solution)/shard_map/reduce_scatter | solution.py:80
  371.8 4.4 copy-start.3
  371.8 106.8 %copy-start.1 = (f32[16,80,8]{1,2,0:T(8,128)S(1)}, f32[16,80,8]{1,2,0:T(8,128)}, u32[]{:S(2)}) copy-start(f32[16,80,8]{1,2,0:T(8,128)} %param.9) | copy-start | bytes 122884
  721.5 6.3 copy-start
Sparse Core Ops, SparseCore 0:
  9.5 340.4 all-gather.2
  373.1 105.4 reduce-scatter.1
where the time goes:
time: 788 us; the launch traced here: 785 us
  waiting for transfers between devices  438 us (56%)
  other arithmetic  161 us (20%)
  blocking collectives  108 us (14%)
  between operations  38.6 us (5%)
  matrix products  21.7 us (3%)
  local copies, waits for them, and re-layouts  17.4 us (2%)
    all_gather x1, waiting for transfers between devices, per_device(): lax.all_gather(expansion_basis, 'img', axis=1, tiled=True)  341 us
    reduce_scatter x1, waiting for transfers between devices, per_device(): lax.psum_scatter(stacked, ('img', 'grp'), scatter_dimension=0, tiled=True)  96 us
    reduce_sum x33, other arithmetic, subspace(): vector = vector - jnp.sum(earlier * vector, axis=1, keepdims=True) * earlier  86.9 us
    all_gather x1, blocking collectives, per_device(): lax.all_gather(solved, ('img', 'grp'), axis=0, tiled=True)  59.5 us
    select_n x3, other arithmetic, subspace(): columns.append(jnp.where(alive, vector / length, jnp.zeros_like(vector)))  52.4 us
    unnamed x1, blocking collectives  48.9 us
    reduce_sum x12, other arithmetic, subspace(): length = jnp.sqrt(jnp.sum(vector * vector, axis=1, keepdims=True))  19.3 us
  transfers between devices with their start and end apart: 2, of which 2 were waited for; matrix products, arithmetic and copies ran while one was open for 0% of the time, Pallas kernels for 0%

commit v1 on v0

--- a/solution.py
+++ b/solution.py
@@ -9,6 +9,28 @@
 KMAX = 8
 ITERS = 3
 HIGH = lax.Precision.HIGHEST
+
+
+def in_order(blocks, dim):
+    dims = list(blocks.shape[1:])
+    dims[dim] *= blocks.shape[0]
+    return jnp.moveaxis(blocks, 0, dim).reshape(dims)
+
+
+def gather_around(shard, axis, dim):
+    peers = lax.axis_size(axis)
+    pairs = [(i, (i + 1) % peers) for i in range(peers)]
+    back = [(b, a) for a, b in pairs]
+    lower, upper = ([], [])
+    for step in range(peers - 1):
+        if step % 2 == 0:
+            lower.append(lax.ppermute(lower[-1] if lower else shard, axis, pairs))
+        else:
+            upper.append(lax.ppermute(upper[-1] if upper else shard, axis, back))
+    blocks = jnp.stack([*lower[::-1], shard, *upper])
+    shift = lax.axis_index(axis) - len(lower)
+    blocks = blocks[(jnp.arange(peers) - shift) % peers]
+    return in_order(blocks, dim)
 
 
 def selector(block_sizes, total, count, width):
@@ -57,9 +79,7 @@
 def per_device(images, expansion_basis, block_sizes, keep_count, start_block):
     rows = images.shape[0]
     coeffs = jnp.dot(
-        images,
-        lax.all_gather(expansion_basis, "img", axis=1, tiled=True),
-        preferred_element_type=jnp.float32,
+        images, gather_around(expansion_basis, "img", 1), preferred_element_type=jnp.float32
     ).astype(jnp.bfloat16)
     samples = coeffs.reshape(2 * rows, S)
     pick = selector(block_sizes, S, L, NMAX)

time: 788 us -> 829 us (1.052)
  local copies, waits for them, and re-layouts: 17.4 us -> 50.8 us
  waiting for transfers between devices: 438 us -> 423 us
  other arithmetic: 161 us -> 175 us
    all_gather x1 -> x0, waiting for transfers between devices: 341 us -> none  [per_device(): lax.all_gather(expansion_basis, 'img', axis=1, tiled=True)]
    ppermute x0 -> x7, waiting for transfers between devices: none -> 327 us  [the longest x4 327 us: gather_around(): lower.append(lax.ppermute(lower[-1] if lower else shard, axis, pairs))]
    gather x0 -> x3, local copies, waits for them, and re-layouts: none -> 23.2 us  [gather_around(): blocks = blocks[(jnp.arange(peers) - shift) % peers]]
    unnamed x1 -> x2, other arithmetic: 0.01 us -> 14.2 us
    unnamed x11 -> x24, local copies, waits for them, and re-layouts: 0.94 us -> 9.82 us
  transfers between devices with their start and end apart: 2 -> 8, of which waited for: 2 -> 5; matrix products, arithmetic and copies ran while one was open for 0% -> 1% of each run, Pallas kernels for 0% -> 0%
where the time goes in v1:
time: 829 us; the launch traced here: 827 us
  waiting for transfers between devices  423 us (51%)
  other arithmetic  175 us (21%)
  blocking collectives  108 us (13%)
  local copies, waits for them, and re-layouts  50.8 us (6%)
  between operations  38.7 us (5%)
  matrix products  21.8 us (3%)
    ppermute x4, waiting for transfers between devices, gather_around(): lower.append(lax.ppermute(lower[-1] if lower else shard, axis, pairs))  327 us
    reduce_scatter x1, waiting for transfers between devices, per_device(): lax.psum_scatter(stacked, ('img', 'grp'), scatter_dimension=0, tiled=True)  96.5 us
    reduce_sum x33, other arithmetic, subspace(): vector = vector - jnp.sum(earlier * vector, axis=1, keepdims=True) * earlier  86.9 us
    all_gather x1, blocking collectives, per_device(): lax.all_gather(solved, ('img', 'grp'), axis=0, tiled=True)  59.5 us
    select_n x3, other arithmetic, subspace(): columns.append(jnp.where(alive, vector / length, jnp.zeros_like(vector)))  52.4 us
    unnamed x1, blocking collectives  48.9 us
    gather x3, local copies, waits for them, and re-layouts, gather_around(): blocks = blocks[(jnp.arange(peers) - shift) % peers]  23.2 us
    reduce_sum x12, other arithmetic, subspace(): length = jnp.sqrt(jnp.sum(vector * vector, axis=1, keepdims=True))  19.3 us
  transfers between devices with their start and end apart: 8, of which 5 were waited for; matrix products, arithmetic and copies ran while one was open for 1% of the time, Pallas kernels for 0%

profile of v1, /device:TPU:14, one launch (start us, length us, event | category | flops | bytes accessed | tf_op | source)
XLA Modules:
  0.0 826.5 jit_solution(2463675826139420620)
XLA Ops:
  8.8 48.5 %collective-permute-done = bf16[9216,120]{0,1:T(8,128)(2,1)S(1)} collective-permute-done((bf16[9216,120]{0,1:T(8,128)(2,1)}, bf16[9216,120]{0,1:T(8,128)(2,1)S(1)}, u32[]{:S(2)}, u32[]{:S(2)}) %collective-permute-start) | collective-permute-done | bytes 2211872 | tf_op jit(solution)/shard_map/ppermute | solution.py:27
  57.3 2.4 collective-permute-start.1
  59.7 93.9 %collective-permute-done.1 = bf16[9216,120]{0,1:T(8,128)(2,1)S(1)} collective-permute-done((bf16[9216,120]{0,1:T(8,128)(2,1)S(1)}, bf16[9216,120]{0,1:T(8,128)(2,1)S(1)}, u32[]{:S(2)}, u32[]{:S(2)}) %collective-permute-start.1) | collective-permute-done | bytes 2211872 | tf_op jit(solution)/shard_map/ppermute | solution.py:27
  157.1 93.6 %collective-permute-done.2 = bf16[9216,120]{0,1:T(8,128)(2,1)} collective-permute-done((bf16[9216,120]{0,1:T(8,128)(2,1)S(1)}, bf16[9216,120]{0,1:T(8,128)(2,1)}, u32[]{:S(2)}, u32[]{:S(2)}) %collective-permute-start.2) | collective-permute-done | bytes 2211872 | tf_op jit(solution)/shard_map/ppermute | solution.py:27
  255.4 90.6 %collective-permute-done.3 = bf16[9216,120]{0,1:T(8,128)(2,1)} collective-permute-done((bf16[9216,120]{0,1:T(8,128)(2,1)}, bf16[9216,120]{0,1:T(8,128)(2,1)}, u32[]{:S(2)}, u32[]{:S(2)}) %collective-permute-start.3) | collective-permute-done | bytes 2211872 | tf_op jit(solution)/shard_map/ppermute | solution.py:27
  353.7 6.3 fusion.43
  360.0 8.5 %gather_fusion.1 = bf16[8,4608,120]{1,2,0:T(8,128)(2,1)} fusion(bf16[8,4608,120]{1,2,0:T(8,128)(2,1)} %get-tuple-element.195, s32[1024]{0:T(1024)S(1)} %pad_clamp_fusion), kind=kCustom, calls=%fused_computation.1 | custom fusion | bytes 17694752 | tf_op jit(solution)/shard_map/gather | solution.py:32
  368.5 8.4 %gather_fusion = bf16[8,4608,120]{1,2,0:T(8,128)(2,1)} fusion(bf16[8,4608,120]{1,2,0:T(8,128)(2,1)} %get-tuple-element.194, s32[1024]{0:T(1024)S(1)} %pad_clamp_fusion), kind=kCustom, calls=%fused_computation | custom fusion | bytes 17694752 | tf_op jit(solution)/shard_map/gather | solution.py:32
  376.8 14.2 %pad_maximum_fusion = bf16[8,9216,120]{1,2,0:T(8,128)(2,1)} fusion(bf16[8,4608,120]{1,2,0:T(8,128)(2,1)} %gather_fusion.1, bf16[8,4608,120]{1,2,0:T(8,128)(2,1)} %gather_fusion), kind=kLoop, calls=%fused_computation.2 | loop fusion | flops 35389440 | bytes 35389440
  391.0 15.0 %fusion.2 = bf16[384,960]{0,1:T(8,128)(2,1)S(1)} fusion(bf16[9216,960]{0,1:T(8,128)(2,1)} %bitcast.336, bf16[384,9216]{1,0:T(8,128)(2,1)} %param.5), kind=kOutput, calls=%fused_computation.15 | convolution fusion | flops 6795141120 | bytes 25509888 | tf_op jit(solution)/shard_map/dot_general | solution.py:81
  406.9 2.5 convolution_convert_fusion
  409.4 2.7 copy.19
  423.6 96.5 %reduce-scatter.2.cloned.1.call-done = f32[1,80,80]{2,1,0:T(8,128)} async-done(((f32[32,80,80]{2,1,0:T(8,128)}), f32[1,80,80]{2,1,0:T(8,128)}) %reduce-scatter.2.cloned.1.call-update) | async-done | bytes 25616 | tf_op jit(solution)/shard_map/reduce_scatter | solution.py:100
  525.1 2.0 multiply_reduce_fusion.84
  527.0 4.4 multiply_reduce_fusion.64
  532.1 4.4 multiply_reduce_fusion.63
  536.5 1.9 multiply_reduce_fusion.80
  539.1 1.9 multiply_reduce_fusion.77
  541.0 5.0 multiply_reduce_fusion.62
  546.7 3.2 multiply_reduce_fusion.61
  549.9 1.9 multiply_reduce_fusion.71
  554.3 2.6 multiply_reduce_fusion.60
  559.4 1.9 multiply_reduce_fusion.58
  562.1 17.5 %broadcast_select_fusion.5 = (f32[1,80,1]{1,2,0:T(1,128)S(1)}, f32[1,80,1]{1,2,0:T(1,128)S(1)}, f32[1,80,1]{1,2,0:T(1,128)S(1)}, f32[1,80,1]{1,2,0:T(1,128)S(1)}...) fusion(pred[]{:T(512)} %bitcast.32, f32[1,80,1]{1,2,0:T(1,128)S(1)} %get-tuple-element.193, ...), kind=kLoop, calls=%fused_computation.50 | loop fusion | flops 5600 | bytes 4947 | tf_op jit(solution)/shard_map/jit(_where)/select_n | solution.py:59
  584.5 2.0 multiply_reduce_fusion.55
  586.4 4.4 multiply_reduce_fusion.35
  591.5 4.4 multiply_reduce_fusion.34
  595.9 1.9 multiply_reduce_fusion.51
  600.4 5.0 multiply_reduce_fusion.33
  606.1 3.2 multiply_reduce_fusion.32
  609.3 1.9 multiply_reduce_fusion.42
  613.6 2.6 multiply_reduce_fusion.31
  618.8 1.9 multiply_reduce_fusion.29
  621.5 17.5 %broadcast_select_fusion.4 = (f32[1,80,1]{1,2,0:T(1,128)S(1)}, f32[1,80,1]{1,2,0:T(1,128)S(1)}, f32[1,80,1]{1,2,0:T(1,128)S(1)}, f32[1,80,1]{1,2,0:T(1,128)S(1)}...) fusion(pred[]{:T(512)} %bitcast.32, f32[1,80,1]{1,2,0:T(1,128)S(1)} %get-tuple-element.158, ...), kind=kLoop, calls=%fused_computation.49 | loop fusion | flops 5600 | bytes 4947 | tf_op jit(solution)/shard_map/jit(_where)/select_n | solution.py:59
  643.8 2.0 multiply_reduce_fusion.26
  645.8 4.4 multiply_reduce_fusion.6
  650.8 4.4 multiply_reduce_fusion.5
  655.2 1.9 multiply_reduce_fusion.22
  659.7 5.0 multiply_reduce_fusion.4
  665.5 3.2 multiply_reduce_fusion.3
  668.6 1.9 multiply_reduce_fusion.13
  673.0 2.6 multiply_reduce_fusion.2
  678.2 1.9 multiply_reduce_fusion
  680.8 17.5 %broadcast_select_fusion.3 = (f32[1,80,1]{1,2,0:T(1,128)S(1)}, f32[1,80,1]{1,2,0:T(1,128)S(1)}, f32[1,80,1]{1,2,0:T(1,128)S(1)}, f32[1,80,1]{1,2,0:T(1,128)S(1)}...) fusion(pred[]{:T(512)} %bitcast.32, f32[1,80,1]{1,2,0:T(1,128)S(1)} %get-tuple-element.123, ...), kind=kLoop, calls=%fused_computation.48 | loop fusion | flops 5600 | bytes 4947 | tf_op jit(solution)/shard_map/jit(_where)/select_n | solution.py:59
  698.3 59.5 %all_gather.6 = bf16[32,80,8]{1,2,0:T(8,128)(2,1)S(1)} all-gather(bf16[1,80,8]{1,2,0:T(8,128)(2,1)S(1)} %convert.8), channel_id=1, replica_groups=mesh['img'=8,'grp'=4] {'img','grp'}, dimensions={0}, use_global_device_ids=true | all-gather | bytes 42240 | tf_op jit(solution)/shard_map/all_gather | solution.py:103
  758.3 4.9 copy.20
  763.1 6.3 reshape.4153
  770.0 48.9 %all-reduce.4 = f32[256]{0:T(256)S(1)} all-reduce(f32[256]{0:T(256)S(1)} %dynamic-update-slice), channel_id=2, replica_groups=mesh['img'=8,'grp'=4] {'img','grp'}, use_global_device_ids=true, to_apply=%add.4 | all-reduce | flops 256 | bytes 2048
  (85 shorter events, 48.8 us)
Async XLA Ops:
  7.2 513.0 %reduce-scatter.2.cloned.1.call-start = ((), (), s32[]{:S(2)}) async-start(), calls=%async_computation.1 | async-start | bytes 1351680 | tf_op jit(solution)/shard_map/reduce_scatter | solution.py:100
  7.2 50.1 %collective-permute-start = (bf16[9216,120]{0,1:T(8,128)(2,1)}, bf16[9216,120]{0,1:T(8,128)(2,1)S(1)}, u32[]{:S(2)}, u32[]{:S(2)}) collective-permute-start(bf16[9216,120]{0,1:T(8,128)(2,1)} %param.6), channel_id=1, source_target_pairs={{0,4},{4,8},{8,12},{12,16},{16,20},{20,24},{24,28},{28,0},{1,5},{5... | collective-permute-start | bytes 6635528 | tf_op jit(solution)/shard_map/ppermute | solution.py:27
  57.3 96.4 %collective-permute-start.1 = (bf16[9216,120]{0,1:T(8,128)(2,1)S(1)}, bf16[9216,120]{0,1:T(8,128)(2,1)S(1)}, u32[]{:S(2)}, u32[]{:S(2)}) collective-permute-start(bf16[9216,120]{0,1:T(8,128)(2,1)S(1)} %collective-permute-done), channel_id=1, source_target_pairs={{0,4},{4,8},{8,12},{12,16},{16,20},{20,24},{24,28},{28,0},{1,5},{5... | collective-permute-start | bytes 6635528 | tf_op jit(solution)/shard_map/ppermute | solution.py:27
  59.7 95.9 %collective-permute-start.4 = (bf16[9216,120]{0,1:T(8,128)(2,1)}, bf16[9216,120]{0,1:T(8,128)(2,1)}, u32[]{:S(2)}, u32[]{:S(2)}) collective-permute-start(bf16[9216,120]{0,1:T(8,128)(2,1)} %param.6), channel_id=1, source_target_pairs={{4,0},{8,4},{12,8},{16,12},{20,16},{24,20},{28,24},{0,28},{5,1},{9... | collective-permute-start | bytes 6635528 | tf_op jit(solution)/shard_map/ppermute | solution.py:29
  153.7 1.4 copy-start.1
  155.0 95.6 %collective-permute-start.2 = (bf16[9216,120]{0,1:T(8,128)(2,1)S(1)}, bf16[9216,120]{0,1:T(8,128)(2,1)}, u32[]{:S(2)}, u32[]{:S(2)}) collective-permute-start(bf16[9216,120]{0,1:T(8,128)(2,1)S(1)} %collective-permute-done.1), channel_id=1, source_target_pairs={{0,4},{4,8},{8,12},{12,16},{16,20},{20,24},{24,28},{28,0},{1,5},{5... | collective-permute-start | bytes 6635528 | tf_op jit(solution)/shard_map/ppermute | solution.py:27
  155.6 98.1 %collective-permute-start.5 = (bf16[9216,120]{0,1:T(8,128)(2,1)}, bf16[9216,120]{0,1:T(8,128)(2,1)}, u32[]{:S(2)}, u32[]{:S(2)}) collective-permute-start(bf16[9216,120]{0,1:T(8,128)(2,1)} %collective-permute-done.4), channel_id=1, source_target_pairs={{4,0},{8,4},{12,8},{16,12},{20,16},{24,20},{28,24},{0,28},{5,1},{9... | collective-permute-start | bytes 6635528 | tf_op jit(solution)/shard_map/ppermute | solution.py:29
  250.6 95.3 %collective-permute-start.3 = (bf16[9216,120]{0,1:T(8,128)(2,1)}, bf16[9216,120]{0,1:T(8,128)(2,1)}, u32[]{:S(2)}, u32[]{:S(2)}) collective-permute-start(bf16[9216,120]{0,1:T(8,128)(2,1)} %collective-permute-done.2), channel_id=1, source_target_pairs={{0,4},{4,8},{8,12},{12,16},{16,20},{20,24},{24,28},{28,0},{1,5},{5... | collective-permute-start | bytes 6635528 | tf_op jit(solution)/shard_map/ppermute | solution.py:27
  253.7 95.8 %copy-start.2 = (bf16[9216,120]{0,1:T(8,128)(2,1)S(1)}, bf16[9216,120]{0,1:T(8,128)(2,1)}, u32[]{:S(2)}) copy-start(bf16[9216,120]{0,1:T(8,128)(2,1)} %copy-done.1) | copy-start | bytes 6635524
  253.7 96.1 %copy-start = (bf16[9216,120]{0,1:T(8,128)(2,1)S(1)}, bf16[9216,120]{0,1:T(8,128)(2,1)}, u32[]{:S(2)}) copy-start(bf16[9216,120]{0,1:T(8,128)(2,1)} %param.6) | copy-start | bytes 6635524
  253.7 99.8 %collective-permute-start.6 = (bf16[9216,120]{0,1:T(8,128)(2,1)}, bf16[9216,120]{0,1:T(8,128)(2,1)S(1)}, u32[]{:S(2)}, u32[]{:S(2)}) collective-permute-start(bf16[9216,120]{0,1:T(8,128)(2,1)} %collective-permute-done.5), channel_id=1, source_target_pairs={{4,0},{8,4},{12,8},{16,12},{20,16},{24,20},{28,24},{0,28},{5,1},{9... | collective-permute-start | bytes 6635528 | tf_op jit(solution)/shard_map/ppermute | solution.py:29
  406.9 7.1 copy-start.5
  406.9 10.3 %copy-start.6 = (s32[16]{0:T(128)S(1)}, s32[16]{0:T(128)}, u32[]{:S(2)}) copy-start(s32[16]{0:T(128)} %param.8) | copy-start | bytes 196
  406.9 113.3 %copy-start.4 = (f32[16,80,8]{1,2,0:T(8,128)S(1)}, f32[16,80,8]{1,2,0:T(8,128)}, u32[]{:S(2)}) copy-start(f32[16,80,8]{1,2,0:T(8,128)} %param.9) | copy-start | bytes 122884
  520.2 249.3 %copy-start.3 = (f32[1,80,80]{2,1,0:T(8,128)S(1)}, f32[1,80,80]{2,1,0:T(8,128)}, u32[]{:S(2)}) copy-start(f32[1,80,80]{2,1,0:T(8,128)} %reduce-scatter.2.cloned.1.call-done) | copy-start | bytes 76804
Sparse Core Ops, SparseCore 0:
  414.1 106.0 reduce-scatter.1
